TPU v7x, 256 devices: a whole 4x4x8 slice. The times are simulated.
256 devices in a mesh: blk: 16 (over z, y_hi), dp: 16 (over y_lo, x, core).
Axes of the slice: x: 4, y: 4 (y_hi: 2, y_lo: 2; y = y_hi * 2 + y_lo), z: 8, core: 2. Of those that a mesh axis runs over, the one named last changes fastest.
Arguments:
- visual_rows: bfloat16 [16, 512, 4096], P('dp', 'blk'), may hold values from -6 to 6
- value_matrix: bfloat16 [16, 512, 512], P('dp', 'blk'), may hold values from -6 to 6
- key_weight: bfloat16 [4096, 512], replicated, may hold values from -1 to 1
- queries: bfloat16 [16, 2048, 4096], P('dp', 'blk'), may hold values from -1024 to 1024
- output_gradient: bfloat16 [16, 2048, 4096], P('dp', 'blk'), may hold values from -6 to 6
- visual_len: int32 [16], P('dp'), may hold values from 128 to 512, as said below
- frame_end: int32 [16, 16], P('dp'), may hold values from 1 to 4, as said below
Outputs:
- attn_out: bfloat16 [16, 2048, 4096], P('dp', 'blk')
- query_grad: bfloat16 [16, 2048, 4096], P('dp', 'blk')
- value_grad: bfloat16 [16, 512, 512], P('dp', 'blk')
- key_weight_grad: float32 [4096, 512], P(('blk', 'dp'))
Inputs may be any that keep to these rules, and one draw needn't show every extreme that they name: `visual_len`: rows 0 to the count minus one of a sample are live; some sample has 512, another 128. `frame_end`: never falling along the text blocks of a sample, 1 for its first block and 4 for its last.
All inputs are finite; a program needn't handle non-finite values.
Results may differ from a plain program's by a relative error of at most 0.02.
Values may be sent and summed in bfloat16 or wider, within the bound.
A program may use at most 128 MiB of HBM per device.

v0:
```python
import jax
import jax.numpy as jnp
from jax import lax
from jax.sharding import PartitionSpec as P

HQ = 32
KEY_HEADS = 4
HEAD_SIZE = 128
TILE = 128
HEADS_PER_KEY = 8


NEGATIVE_FILLER = -1e30


def local(visual_rows, value_matrix, key_weight, queries, output_gradient, visual_len, frame_end):
    head_span_width = KEY_HEADS * HEAD_SIZE
    text_row_count = queries.shape[1]
    cycle_size = lax.axis_size("blk")
    cycle_index = lax.axis_index("blk")
    scale = HEAD_SIZE ** (-0.5)
    visual = visual_rows[0]
    key_rows = jnp.dot(visual, key_weight, preferred_element_type=jnp.float32).astype(jnp.bfloat16)
    key_values = jnp.concatenate([key_rows, value_matrix[0]], axis=1)
    all_rows = visual.shape[0] * cycle_size
    query_matrix = queries[0].reshape(text_row_count, KEY_HEADS, HEADS_PER_KEY, HEAD_SIZE)
    gradient_rows = output_gradient[0].reshape(text_row_count, KEY_HEADS, HEADS_PER_KEY, HEAD_SIZE)
    tile_count = text_row_count // TILE
    frame_tiles = lax.dynamic_slice_in_dim(frame_end[0], cycle_index * tile_count, tile_count, 0)
    limits = jnp.minimum(
        visual_len[0], TILE * jnp.repeat(frame_tiles, TILE, total_repeat_length=text_row_count)
    )
    gathered = lax.all_gather(key_values, "blk", axis=0, tiled=True)
    key_portion = gathered[:, :head_span_width].reshape(all_rows, KEY_HEADS, HEAD_SIZE)
    value_portion = gathered[:, head_span_width:].reshape(all_rows, KEY_HEADS, HEAD_SIZE)
    raw_scores = jnp.einsum(
        "tkgd,rkd->kgrt", query_matrix, key_portion, preferred_element_type=jnp.float32
    )
    positions = jnp.arange(all_rows, dtype=jnp.int32)
    live_mask = positions[:, None] < limits[None, :]
    scores = jnp.where(live_mask, raw_scores * scale, NEGATIVE_FILLER)
    row_peak = jnp.max(scores, axis=2, keepdims=True)
    shifted = jnp.where(live_mask, jnp.exp(scores - row_peak), 0.0)
    probs = shifted / jnp.sum(shifted, axis=2, keepdims=True)
    weights = probs.astype(jnp.bfloat16)
    attn_out = jnp.einsum(
        "kgrt,rkd->tkgd", weights, value_portion, preferred_element_type=jnp.float32
    ).astype(jnp.bfloat16)
    grad_delta = jnp.einsum(
        "tkgd,tkgd->kgt", gradient_rows.astype(jnp.float32), attn_out.astype(jnp.float32)
    )
    dprobs = jnp.einsum(
        "tkgd,rkd->kgrt", gradient_rows, value_portion, preferred_element_type=jnp.float32
    )
    dscores = (probs * (dprobs - grad_delta[:, :, None, :]) * scale).astype(jnp.bfloat16)
    query_acc = jnp.einsum(
        "kgrt,rkd->tkgd", dscores, key_portion, preferred_element_type=jnp.float32
    )
    key_grads = jnp.einsum(
        "kgrt,tkgd->rkd", dscores, query_matrix, preferred_element_type=jnp.float32
    )
    value_grads = jnp.einsum(
        "kgrt,tkgd->rkd", weights, gradient_rows, preferred_element_type=jnp.float32
    )
    row_sums = jnp.concatenate(
        [
            key_grads.reshape(all_rows, head_span_width),
            value_grads.reshape(all_rows, head_span_width),
        ],
        axis=1,
    )
    own_sums = lax.psum_scatter(
        row_sums.astype(jnp.bfloat16), "blk", scatter_dimension=0, tiled=True
    ).astype(jnp.float32)
    value_grad = own_sums[:, head_span_width:].astype(jnp.bfloat16)
    key_grad = own_sums[:, :head_span_width].astype(jnp.bfloat16)
    partial_grad = jnp.einsum("rc,rk->ck", visual, key_grad, preferred_element_type=jnp.float32)
    weight_grad = lax.psum_scatter(partial_grad, ("blk", "dp"), scatter_dimension=0, tiled=True)
    return (
        attn_out.reshape(1, text_row_count, HQ * HEAD_SIZE),
        query_acc.astype(jnp.bfloat16).reshape(1, text_row_count, HQ * HEAD_SIZE),
        value_grad[None],
        weight_grad,
    )


def solution(mesh):
    return jax.shard_map(
        local,
        mesh=mesh,
        in_specs=(
            P("dp", "blk", None),
            P("dp", "blk", None),
            P(),
            P("dp", "blk", None),
            P("dp", "blk", None),
            P("dp"),
            P("dp", None),
        ),
        out_specs=(
            P("dp", "blk", None),
            P("dp", "blk", None),
            P("dp", "blk", None),
            P(("blk", "dp"), None),
        ),
        check_vma=False,
    )
```

profile of v0, /device:TPU:1, one launch (start us, length us, event | category | flops | bytes accessed | tf_op | source)
XLA Modules:
  0.0 1636.5 jit_solution(12790668743598154895)
XLA Ops:
  7.3 0.9 copy-done
  8.1 3.0 convolution_convert_fusion.2
  12.5 1.3 copy.60
  14.1 1.7 copy.31
  17.1 73.0 %all-gather.2.cloned.1.call-done = bf16[512,1024]{1,0:T(8,128)(2,1)} async-done(((bf16[32,1024]{1,0:T(8,128)(2,1)}), bf16[512,1024]{1,0:T(8,128)(2,1)}) %all-gather.2.cloned.1.call-update) | async-done | bytes 1048592 | tf_op jit(solution)/shard_map/all_gather | solution.py:33
  90.1 1.3 fusion.24
  92.0 7.9 fusion.26
  99.9 4.5 fusion.12
  104.4 2.3 fusion.14
  106.7 2.5 bitcast_convert_fusion
  109.2 2.4 copy.45
  111.6 1.6 multiply_reduce_fusion
  113.1 1.0 copy.46
  114.2 5.7 fusion.3
  119.9 1.5 fusion.13
  122.3 1.1 pad_maximum_fusion
  123.7 200.3 %reduce-scatter.5.cloned.1.call-done = bf16[32,1024]{1,0:T(8,128)(2,1)} async-done(((bf16[512,1024]{1,0:T(8,128)(2,1)}), bf16[32,1024]{1,0:T(8,128)(2,1)}) %reduce-scatter.5.cloned.1.call-update) | async-done | bytes 65552 | tf_op jit(solution)/shard_map/reduce_scatter | solution.py:72
  323.9 5.3 convolution_bitcast_fusion
  329.2 9.0 copy.58
  338.2 1.0 copy-done.4
  339.3 3.0 convolution_convert_fusion
  342.3 1.3 copy.35
  343.6 1.3 copy.34
  345.6 1284.5 %reduce-scatter.7.cloned.1.call-done = f32[16,512]{1,0:T(8,128)} async-done(((f32[4096,512]{1,0:T(8,128)}), f32[16,512]{1,0:T(8,128)}) %reduce-scatter.7.cloned.1.call-update) | async-done | bytes 32784
  (42 shorter events, 4.0 us)
Async XLA Ops:
  7.2 1.0 copy-start
  7.2 4.0 copy-start.12
  7.2 5.3 copy-start.6
  7.2 6.6 copy-start.7
  7.2 82.9 %all-gather.2.cloned.1.call-start = ((), (), s32[]{:S(2)}) async-start(), calls=%async_computation.2 | async-start | bytes 1114112 | tf_op jit(solution)/shard_map/all_gather | solution.py:33
  11.1 4.6 copy-start.13
  11.8 312.1 %reduce-scatter.5.cloned.1.call-start = ((), (), s32[]{:S(2)}) async-start(), calls=%async_computation.3 | async-start | bytes 1114112 | tf_op jit(solution)/shard_map/reduce_scatter | solution.py:72
  91.5 15.2 copy-start.5
  92.0 7.9 copy-start.3
  99.9 4.5 copy-start.9
  114.1 5.7 copy-start.8
  119.9 1.9 copy-start.1
  119.9 2.2 copy-start.10
  123.4 1506.6 %reduce-scatter.7.cloned.1.call-start = ((), (), s32[]{:S(2)}) async-start(), calls=%async_computation.4 | async-start | bytes 8421376
  338.2 1.0 copy-start.4
  339.3 4.4 copy-start.2
  342.3 2.6 copy-start.11
Sparse Core Ops, SparseCore 0:
  11.9 78.1 all-gather.1
  123.5 200.3 reduce-scatter.4
  338.4 1291.5 reduce-scatter.6
where the time goes:
time: 1640 us
  waiting for transfers between devices  1560 us (95%)
  matrix products  31.2 us (2%)
  local copies, waits for them, and re-layouts  23.5 us (1%)
    unnamed x4, waiting for transfers between devices  1280 us
    reduce_scatter x1, waiting for transfers between devices, local(): lax.psum_scatter(row_sums.astype(jnp.bfloat16), 'blk', scatter_dimension=...  200 us
    all_gather x1, waiting for transfers between devices, local(): gathered = lax.all_gather(key_values, 'blk', axis=0, tiled=True)  73 us
  transfers between devices with their start and end apart: 3, of which 3 were waited for; matrix products, arithmetic and copies ran while one was open for 1% of the time, Pallas kernels for 0%

commit v1 on v0

v1 whole, which is shorter than its diff:
```python
import functools
import math

import jax
import jax.numpy as jnp
from jax import lax
from jax.experimental import pallas as pl
from jax.experimental.pallas import tpu as pltpu
from jax.sharding import PartitionSpec as P

HEADS = 4
GROUP = 8
D = 128
TILE = 128
ROWS = 32
SCALE = D ** (-0.5)
EXP2_SCALE = SCALE * math.log2(math.e)
FILLER = -1e30
MESH = pl.DeviceIdType.MESH
F32 = jnp.float32
BF16 = jnp.bfloat16
VM = pl.BlockSpec(memory_space=pltpu.VMEM)


def ring_position():
    b = lax.axis_index("blk")
    z, y = b // 2, b % 2
    nz = lax.axis_size("blk") // 2

    def at(step, yy):
        return lax.rem(z + step + nz, nz) * 2 + yy

    return b, z, y, nz, at


def copy_to(src, dst, send, recv, axis, index):
    c = pltpu.make_async_remote_copy(
        src_ref=src, dst_ref=dst, send_sem=send, recv_sem=recv,
        device_id={axis: index}, device_id_type=MESH)
    c.start()
    return c


class Gather:
    def __init__(self, bufs, send, recv, ysend, yrecv):
        self.bufs, self.send, self.recv = bufs, send, recv
        self.ysend, self.yrecv = ysend, yrecv
        self.b, self.z, self.y, self.nz, self.at = ring_position()
        self.copies = []
        self.ycopies = {}
        self.hops = {}

    def length(self, x, way):
        return self.nz // 2 if x == way else self.nz // 2 - 1

    def go(self, x, mine, way, hop):
        step = 1 if way == 0 else -1
        yy = self.y if mine == 0 else 1 - self.y
        slot = self.at(-step * (hop - 1), yy)
        ref = self.bufs[x].at[slot]
        c = copy_to(ref, ref, self.send.at[x, mine, way, hop - 1],
                    self.recv.at[x, mine, way, hop - 1], "blk", self.at(step, self.y))
        self.hops[x, mine, way, hop] = c
        self.copies.append(c)

    def start(self, x):
        ref = self.bufs[x].at[self.b]
        c = copy_to(ref, ref, self.ysend.at[x], self.yrecv.at[x], "blk", self.at(0, 1 - self.y))
        self.ycopies[x] = c
        self.copies.append(c)
        for way in (0, 1):
            self.go(x, 0, way, 1)

    def across(self, x):
        self.ycopies[x].wait_recv()
        for way in (0, 1):
            self.go(x, 1, way, 1)

    def advance(self, x, mine, hop):
        for way in (0, 1):
            n = self.length(x, way)
            if hop <= n:
                self.hops[x, mine, way, hop].wait_recv()
                if hop < n:
                    self.go(x, mine, way, hop + 1)

    def run(self):
        for hop in range(1, self.nz // 2 + 1):
            for x in (0, 1):
                self.advance(x, 0, hop)
                if hop == 1:
                    self.across(x)
            for x in (0, 1):
                self.advance(x, 1, hop)

    def finish(self):
        for c in self.copies:
            c.wait_send()


class Scatter:
    def __init__(self, parts, inbox, outbox, yin, yout, send, recv, ysend, yrecv):
        self.parts, self.inbox, self.outbox = parts, inbox, outbox
        self.yin, self.yout = yin, yout
        self.send, self.recv, self.ysend, self.yrecv = send, recv, ysend, yrecv
        self.b, self.z, self.y, self.nz, self.at = ring_position()
        self.copies = []
        self.hops = {}

    def length(self, x, way):
        return self.nz // 2 if x == way else self.nz // 2 - 1

    def go(self, x, way, hop):
        step = 1 if way == 0 else -1
        n = self.length(x, way)
        first = self.at(step * (n - hop + 1), 0)
        rows = self.parts[x].at[pl.ds(first, 2)]
        if hop == 1:
            src = rows
        else:
            src = self.outbox.at[x, way, hop - 2]
            src[...] = (rows[...].astype(F32) + self.inbox[x, way, hop - 2].astype(F32)).astype(BF16)
        c = copy_to(src, self.inbox.at[x, way, hop - 1], self.send.at[x, way, hop - 1],
                    self.recv.at[x, way, hop - 1], "blk", self.at(step, self.y))
        self.hops[x, way, hop] = c
        self.copies.append(c)

    def start(self, x):
        for way in (0, 1):
            self.go(x, way, 1)

    def advance(self, x, hop):
        for way in (0, 1):
            n = self.length(x, way)
            if hop <= n:
                self.hops[x, way, hop].wait_recv()
                if hop < n:
                    self.go(x, way, hop + 1)

    def sum_at(self, x, slot, yy):
        total = self.parts[x][slot].astype(F32)
        for way in (0, 1):
            total += self.inbox[x, way, self.length(x, way) - 1, yy].astype(F32)
        return total

    def across(self, x):
        other = 1 - self.y
        self.yout[x] = self.sum_at(x, self.at(0, other), other).astype(BF16)
        c = copy_to(self.yout.at[x], self.yin.at[x], self.ysend.at[x], self.yrecv.at[x],
                    "blk", self.at(0, other))
        self.copies.append(c)
        return c

    def run(self):
        for x in (0, 1):
            self.start(x)
        for hop in range(1, self.nz // 2 + 1):
            for x in (0, 1):
                self.advance(x, hop)
        return [self.across(x) for x in (0, 1)]

    def result(self, x, c):
        c.wait_recv()
        return self.sum_at(x, self.b, self.y) + self.yin[x].astype(F32)

    def finish(self):
        for c in self.copies:
            c.wait_send()


def greet(axis_peers):
    barrier = pltpu.get_barrier_semaphore()
    for axis, index in axis_peers:
        pl.semaphore_signal(barrier, inc=1, device_id={axis: index}, device_id_type=MESH)
    return lambda: pl.semaphore_wait(barrier, len(axis_peers))


def others(axis):
    n = lax.axis_size(axis)
    me = lax.axis_index(axis)
    return [(i, lax.rem(me + i, n)) for i in range(1, n)]


def gather_kernel(visual, values, weight, k_out, v_out, vis_out,
                  send, recv, ysend, yrecv, vsend, vrecv, local):
    b = lax.axis_index("blk")
    n = lax.axis_size("blk")
    width = visual.shape[1] // n
    ready = greet([("blk", j) for _, j in others("blk")])
    g = Gather((v_out, k_out), send, recv, ysend, yrecv)
    v_out[b] = values[...]
    k_out[b] = jnp.dot(visual[...], weight[...], preferred_element_type=F32).astype(BF16)
    ready()
    g.start(0)
    g.start(1)
    own = pltpu.make_async_copy(
        visual.at[:, pl.ds(pl.multiple_of(b * width, width), width)], vis_out.at[b], local)
    own.start()
    moves = []
    for i, j in others("blk"):
        moves.append(copy_to(
            visual.at[:, pl.ds(pl.multiple_of(j * width, width), width)], vis_out.at[b],
            vsend.at[i - 1], vrecv.at[i - 1], "blk", j))
    g.run()
    g.finish()
    own.wait()
    for c in moves:
        c.wait_send()
        c.wait_recv()


def dot(a, b, dims):
    return lax.dot_general(a, b, (dims, ((), ())), preferred_element_type=F32)


def attention_kernel(length, frames, q_ref, g_ref, k_ref, v_ref, o_ref, dq_ref, dk_ref, dv_ref):
    tile = lax.axis_index("blk")
    limit = jnp.minimum(length[0], TILE * frames[0, tile])
    k, v = k_ref[...], v_ref[...]
    k_t, v_t = k.T, v.T
    rows = k.shape[0]
    dk = dv = None
    for p in range(GROUP // 2):
        at = [slice((2 * p + i) * D, (2 * p + i + 1) * D) for i in (0, 1)]
        q = jnp.concatenate([q_ref[:, s] for s in at], axis=0)
        g = jnp.concatenate([g_ref[:, s] for s in at], axis=0)
        g_t = g.T
        s = dot(k, q, ((1,), (1,)))
        live = lax.broadcasted_iota(jnp.int32, s.shape, 0) < limit
        s = jnp.where(live, s, FILLER)
        peak = jnp.max(s, axis=0, keepdims=True)
        e = jnp.exp2((s - peak) * EXP2_SCALE)
        probs = e * (1.0 / jnp.sum(e, axis=0, keepdims=True))
        w = probs.astype(BF16)
        o_t = dot(v_t, w, ((1,), (0,))).astype(BF16).astype(F32)
        delta = jnp.sum(g_t.astype(F32) * o_t, axis=0, keepdims=True)
        dp = dot(v, g_t, ((1,), (0,)))
        ds = (probs * ((dp - delta) * SCALE)).astype(BF16)
        dq_t = dot(k_t, ds, ((1,), (0,)))
        o = o_t.T.astype(BF16)
        dq = dq_t.T.astype(BF16)
        for i in (0, 1):
            o_ref[:, at[i]] = o[i * D:(i + 1) * D]
            dq_ref[:, at[i]] = dq[i * D:(i + 1) * D]
        dv_p = dot(w, g, ((1,), (0,)))
        dk_p = dot(ds, q, ((1,), (0,)))
        dv = dv_p if dv is None else dv + dv_p
        dk = dk_p if dk is None else dk + dk_p
    dk_ref[...] = dk.astype(BF16)
    dv_ref[...] = dv.astype(BF16)


def reduce_kernel(dk, dv, vis, dv_out, dw_out,
                  inbox, outbox, yin, yout, kg0, kg1, part, landed,
                  send, recv, ysend, yrecv, gsend, grecv, gysend, gyrecv, wsend, wrecv):
    b, z, y, nz, at = ring_position()
    d = lax.axis_index("dp")
    n = lax.axis_size("dp")
    ready = greet([("blk", at(1, y)), ("blk", at(-1, y)), ("blk", at(0, 1 - y))]
                  + [("dp", j) for _, j in others("dp")])
    ready()
    r = Scatter((dk, dv), inbox, outbox, yin, yout, send, recv, ysend, yrecv)
    ck, cv = r.run()
    key_grad = r.result(0, ck).astype(BF16)
    half = key_grad.shape[1] // 2
    g = Gather((kg0, kg1), gsend, grecv, gysend, gyrecv)
    kg0[b] = key_grad[:, :half]
    g.start(0)
    kg1[b] = key_grad[:, half:]
    g.start(1)
    dv_out[...] = r.result(1, cv).astype(BF16)
    vis_t = vis[...].reshape(-1, vis.shape[2]).T
    g.run()
    for i, kg in enumerate((kg0, kg1)):
        w = dot(vis_t, kg[...].reshape(-1, half), ((1,), (0,)))
        part[:, :, i * half:(i + 1) * half] = w.astype(BF16).reshape(n, -1, half)
    moves = []
    for i, j in others("dp"):
        moves.append(copy_to(part.at[j], landed.at[i - 1], wsend.at[i - 1], wrecv.at[i - 1], "dp", j))
    total = part[d].astype(F32)
    for i, c in enumerate(moves):
        c.wait_recv()
        total += landed[i].astype(F32)
    dw_out[...] = total
    r.finish()
    g.finish()
    for c in moves:
        c.wait_send()


def local(visual_rows, value_matrix, key_weight, queries, output_gradient, visual_len, frame_end):
    nb, nd = lax.axis_size("blk"), lax.axis_size("dp")
    hop = nb // 4
    width = HEADS * D
    features = visual_rows.shape[2]
    per = features // nb
    text = queries.shape[1]
    dma = pltpu.SemaphoreType.DMA
    gather_sems = [dma((2, 2, 2, hop)), dma((2, 2, 2, hop)), dma((2,)), dma((2,))]

    keys, values, vis = pl.pallas_call(
        gather_kernel,
        out_shape=(
            jax.ShapeDtypeStruct((nb, ROWS, width), BF16),
            jax.ShapeDtypeStruct((nb, ROWS, width), BF16),
            jax.ShapeDtypeStruct((nb, ROWS, per), BF16),
        ),
        in_specs=[VM] * 3,
        out_specs=(VM,) * 3,
        scratch_shapes=gather_sems + [dma((nb - 1,)), dma((nb - 1,)), dma],
        compiler_params=pltpu.CompilerParams(collective_id=0, has_side_effects=True),
        name="gather_rows",
    )(visual_rows[0], value_matrix[0], key_weight)

    total = nb * ROWS
    col = lambda rows, c: pl.BlockSpec((rows, c), lambda i: (0, i))
    smem = pl.BlockSpec(memory_space=pltpu.SMEM)
    attn_out, query_grad, dk, dv = pl.pallas_call(
        attention_kernel,
        grid=(HEADS,),
        out_shape=(
            jax.ShapeDtypeStruct((text, queries.shape[2]), BF16),
            jax.ShapeDtypeStruct((text, queries.shape[2]), BF16),
            jax.ShapeDtypeStruct((total, width), BF16),
            jax.ShapeDtypeStruct((total, width), BF16),
        ),
        in_specs=[smem, smem, col(text, GROUP * D), col(text, GROUP * D), col(total, D), col(total, D)],
        out_specs=(col(text, GROUP * D), col(text, GROUP * D), col(total, D), col(total, D)),
        compiler_params=pltpu.CompilerParams(vmem_limit_bytes=48 << 20),
        name="attention",
    )(visual_len, frame_end, queries[0], output_gradient[0],
      keys.reshape(total, width), values.reshape(total, width))

    value_grad, weight_grad = pl.pallas_call(
        reduce_kernel,
        out_shape=(
            jax.ShapeDtypeStruct((ROWS, width), BF16),
            jax.ShapeDtypeStruct((per // nd, width), F32),
        ),
        in_specs=[VM] * 3,
        out_specs=(VM,) * 2,
        scratch_shapes=[
            pltpu.VMEM((2, 2, hop, 2, ROWS, width), BF16),
            pltpu.VMEM((2, 2, hop - 1, 2, ROWS, width), BF16),
            pltpu.VMEM((2, ROWS, width), BF16),
            pltpu.VMEM((2, ROWS, width), BF16),
            pltpu.VMEM((nb, ROWS, width // 2), BF16),
            pltpu.VMEM((nb, ROWS, width // 2), BF16),
            pltpu.VMEM((nd, per // nd, width), BF16),
            pltpu.VMEM((nd - 1, per // nd, width), BF16),
            dma((2, 2, hop)), dma((2, 2, hop)), dma((2,)), dma((2,)),
        ] + gather_sems + [dma((nd - 1,)), dma((nd - 1,))],
        compiler_params=pltpu.CompilerParams(collective_id=1, has_side_effects=True),
        name="reduce_rows",
    )(dk.reshape(nb, ROWS, width), dv.reshape(nb, ROWS, width), vis)
    return attn_out[None], query_grad[None], value_grad[None], weight_grad


def solution(mesh):
    return jax.shard_map(
        local,
        mesh=mesh,
        in_specs=(
            P("dp", "blk", None),
            P("dp", "blk", None),
            P(),
            P("dp", "blk", None),
            P("dp", "blk", None),
            P("dp"),
            P("dp", None),
        ),
        out_specs=(
            P("dp", "blk", None),
            P("dp", "blk", None),
            P("dp", "blk", None),
            P(("blk", "dp"), None),
        ),
        check_vma=False,
    )
```

time: 1640 us -> 110 us (0.07)
  waiting for transfers between devices: 1560 us -> 0 us
  Pallas kernels: 0 us -> 102 us
  matrix products: 31.2 us -> 0 us
  local copies, waits for them, and re-layouts: 23.5 us -> 6.41 us
    unnamed x4 -> x0, waiting for transfers between devices: 1280 us -> none
    reduce_scatter x1 -> x0, waiting for transfers between devices: 200 us -> none  [local(): lax.psum_scatter(row_sums.astype(jnp.bfloat16), 'blk', scatter_dimension=...]
    pallas_call x0 -> x3, Pallas kernels: none -> 102 us  [the longest x1 51.9 us: local(): pl.pallas_call(reduce_kernel, out_shape=(jax.ShapeDtypeStruct((ROWS, widt...]
    all_gather x1 -> x0, waiting for transfers between devices: 73 us -> none  [local(): gathered = lax.all_gather(key_values, 'blk', axis=0, tiled=True)]
    dot_general x7 -> x0, matrix products: 23.3 us -> none  [the longest x1 5.71 us: local(): jnp.einsum('tkgd,rkd->kgrt', gradient_rows, value_portion, preferred_elem...]
  transfers between devices with their start and end apart: 3 -> 0, of which waited for: 3 -> 0; matrix products, arithmetic and copies ran while one was open for 1% -> 0% of each run, Pallas kernels for 0% -> 0%
where the time goes in v1:
time: 110 us; the launch traced here: 109 us
  Pallas kernels  102 us (93%)
  local copies, waits for them, and re-layouts  6.41 us (6%)
  between operations  1.5 us (1%)
    pallas_call x1, Pallas kernels, local(): pl.pallas_call(reduce_kernel, out_shape=(jax.ShapeDtypeStruct((ROWS, widt...  51.9 us
    pallas_call x1, Pallas kernels, local(): pl.pallas_call(gather_kernel, out_shape=(jax.ShapeDtypeStruct((nb, ROWS,...  32.7 us
    pallas_call x1, Pallas kernels, local(): pl.pallas_call(attention_kernel, grid=(HEADS,), out_shape=(jax.ShapeDtype...  17 us
    unnamed x16, local copies, waits for them, and re-layouts  6.41 us

profile of v1, /device:TPU:1, one launch (start us, length us, event | category | flops | bytes accessed | tf_op | source)
XLA Modules:
  0.0 109.4 jit_solution(16170525560540104798)
XLA Ops:
  0.6 0.0 copy-start.6
  0.6 0.0 copy-start.1
  0.7 0.0 copy-start
  1.5 32.7 %gather_rows.1 = (bf16[16,32,512]{2,1,0:T(8,128)(2,1)}, bf16[16,32,512]{2,1,0:T(8,128)(2,1)}, bf16[16,32,256]{2,1,0:T(8,128)(2,1)}) custom-call(bf16[32,4096]{1,0:T(8,128)(2,1)} %bitcast.17, bf16[32,512]{1,0:T(8,128)(2,1)} %bitcast.18, bf16[4096,512]{1,0:T(8,128)(2,1)} %weight.1), custom_call_target="tpu_custom_call" | custom-call | tf_op jit(solution)/shard_map/gather_rows/pallas_call | solution.py:301
  34.1 0.0 copy-done.6
  34.2 0.0 copy-done.1
  34.2 0.0 copy-done
  34.2 0.0 copy-start.4
  34.2 1.0 copy-done.4
  35.2 0.0 copy-start.5
  35.2 1.0 copy-done.5
  36.3 17.0 %attention.1 = (bf16[128,4096]{1,0:T(8,128)(2,1)}, bf16[128,4096]{1,0:T(8,128)(2,1)}, bf16[512,512]{1,0:T(8,128)(2,1)S(1)}, bf16[512,512]{1,0:T(8,128)(2,1)S(1)}) custom-call(s32[1]{0:T(128)S(6)} %copy.13.length, s32[1,16]{1,0:T(1,128)S(1)} %copy-done.6, bf16[128,4096]{1,0:T(8,128)(2,1)S(1)} %bitcast.11, bf16[128,4096]{1,0:T(8,128)(2,1)S(1)} %bitcast.12, ...), custom_call_target="tpu_custom_call" | custom-call | tf_op jit(solution)/shard_map/attention/pallas_call | solution.py:318
  53.2 0.0 copy-start.2
  53.2 0.8 copy-done.2
  54.0 0.0 copy-start.3
  54.0 0.8 copy-done.3
  54.8 51.9 %reduce_rows.1 = (bf16[32,512]{1,0:T(8,128)(2,1)}, f32[16,512]{1,0:T(8,128)}) custom-call(bf16[16,32,512]{2,1,0:T(8,128)(2,1)} %bitcast.13, bf16[16,32,512]{2,1,0:T(8,128)(2,1)} %bitcast.14, bf16[16,32,256]{2,1,0:T(8,128)(2,1)} %get-tuple-element.19.vis), custom_call_target="tpu_custom_call" | custom-call | tf_op jit(solution)/shard_map/reduce_rows/pallas_call | solution.py:334
  106.7 1.4 %copy.14 = bf16[1,32,512]{2,1,0:T(8,128)(2,1)} copy(bf16[1,32,512]{2,1,0:T(8,128)(2,1)} %bitcast.19) | data formatting | bytes 65536
  108.0 1.4 %copy.15 = f32[16,512]{1,0:T(8,128)} copy(f32[16,512]{1,0:T(8,128)} %get-tuple-element.29) | data formatting | bytes 65536
Async XLA Ops:
  0.6 33.5 %copy-start.6 = (s32[1,16]{1,0:T(1,128)S(1)}, s32[1,16]{1,0:T(1,128)}, u32[]{:S(2)}) copy-start(s32[1,16]{1,0:T(1,128)} %frames.1) | copy-start | bytes 196
  0.6 33.5 %copy-start.1 = (bf16[1,128,4096]{2,1,0:T(8,128)(2,1)S(1)}, bf16[1,128,4096]{2,1,0:T(8,128)(2,1)}, u32[]{:S(2)}) copy-start(bf16[1,128,4096]{2,1,0:T(8,128)(2,1)} %param.11) | copy-start | bytes 3145732
  0.7 33.5 %copy-start = (bf16[1,128,4096]{2,1,0:T(8,128)(2,1)S(1)}, bf16[1,128,4096]{2,1,0:T(8,128)(2,1)}, u32[]{:S(2)}) copy-start(bf16[1,128,4096]{2,1,0:T(8,128)(2,1)} %param.10) | copy-start | bytes 3145732
  34.2 1.0 copy-start.4
  35.2 1.0 copy-start.5
  53.2 0.8 copy-start.2
  54.0 0.8 copy-start.3

commit v2 on v0

v2 whole, which is shorter than its diff:
```python
import math

import jax
import jax.numpy as jnp
from jax import lax
from jax.experimental import pallas as pl
from jax.experimental.pallas import tpu as pltpu
from jax.sharding import PartitionSpec as P

HEADS = 4
GROUP = 8
D = 128
SPAN = GROUP * D
TILE = 128
ROWS = 32
SCALE = D ** (-0.5)
EXP2_SCALE = SCALE * math.log2(math.e)
FILLER = -1e30
MESH = pl.DeviceIdType.MESH
F32 = jnp.float32
BF16 = jnp.bfloat16


def dot(a, b, dims):
    return lax.dot_general(a, b, (dims, ((), ())), preferred_element_type=F32)


def near_first(n):
    return sorted(range(1, n), key=lambda i: min(i, n - i))


def kernel(length, frames, visual_hbm, values_hbm, weight_hbm, queries_hbm, grads_hbm,
           o_hbm, dq_hbm, dv_out, dw_out,
           visual, values, weight, q_ref, g_ref, o_ref, dq_ref, bias,
           kv, part, yin, half, zin, kg, vis, wpart, landed,
           load, weight_load, store,
           zsend, zrecv, fsend, frecv, vsend, vrecv,
           ysend, yrecv, hsend, hrecv, ksend, krecv, wsend, wrecv):
    b = lax.axis_index("blk")
    d = lax.axis_index("dp")
    nb, nd = lax.axis_size("blk"), lax.axis_size("dp")
    nz = nb // 2
    z, y = b // 2, b % 2
    per = visual.shape[1] // nb

    def zmod(i):
        return lax.rem(z + i, nz)

    def zpeer(i):
        return zmod(i) * 2 + y

    partner = b + 1 - 2 * y
    peers = [(i, s) for i in [0] + near_first(nz) for s in (0, 1) if i or s]
    sent = []

    def send(src, dst, ssem, rsem, axis, index):
        c = pltpu.make_async_remote_copy(
            src_ref=src, dst_ref=dst, send_sem=ssem, recv_sem=rsem,
            device_id={axis: index}, device_id_type=MESH)
        c.start()
        sent.append(c)
        return c

    def side(s):
        return y if s == 0 else 1 - y

    def at(i, s):
        return zmod(i) * 2 + side(s)

    loads = []
    for i, (src, dst) in enumerate(((visual_hbm, visual), (values_hbm, values))):
        loads.append(pltpu.make_async_copy(src, dst, load.at[i]))
        loads[-1].start()
    wloads = []
    for j in range(HEADS):
        cols = pl.ds(j * D, D)
        wloads.append(pltpu.make_async_copy(weight_hbm.at[:, cols], weight.at[:, cols], weight_load.at[j]))
        wloads[-1].start()
    for i, (src, dst) in enumerate(((queries_hbm, q_ref), (grads_hbm, g_ref))):
        loads.append(pltpu.make_async_copy(src, dst, load.at[2 + i]))
        loads[-1].start()

    barrier = pltpu.get_barrier_semaphore()
    for i, s in peers:
        pl.semaphore_signal(barrier, inc=1, device_id={"blk": at(i, s)}, device_id_type=MESH)
    for i in range(1, nd):
        pl.semaphore_signal(barrier, inc=1, device_id={"dp": lax.rem(d + i, nd)}, device_id_type=MESH)

    limit = jnp.minimum(length[0], TILE * frames[0, b])
    r = lax.broadcasted_iota(jnp.int32, bias.shape, 0)
    row = ((r & (nz * ROWS - 1)) // ROWS) * (2 * ROWS) + (r // (nz * ROWS)) * ROWS + (r & (ROWS - 1))
    bias[...] = jnp.where(row < limit, 0.0, FILLER)

    zcopies, fcopies = {}, {}

    def project(j):
        wloads[j].wait()
        cols = slice(j * D, (j + 1) * D)
        key = jnp.dot(visual[...], weight[:, cols], preferred_element_type=F32)
        kv[j, y, z, :, :D] = key.astype(BF16)
        kv[j, y, z, :, D:] = values[:, cols]

    def gather(j):
        ref = kv.at[j, y, z]
        fcopies[j, 0] = send(ref, ref, fsend.at[j, 0], frecv.at[j, 0], "blk", partner)
        for i in near_first(nz):
            zcopies[j, i] = send(ref, ref, zsend.at[j, i - 1], zrecv.at[j, i - 1], "blk", zpeer(i))

    def forward(j):
        for i in near_first(nz):
            zcopies[j, i].wait_recv()
            ref = kv.at[j, y, zmod(nz - i)]
            fcopies[j, i] = send(ref, ref, fsend.at[j, i], frecv.at[j, i], "blk", partner)

    def arrive(j):
        for i in range(nz):
            fcopies[j, i].wait_recv()

    vcopies = []

    def exchange():
        for n, (i, s) in enumerate(peers):
            t = at(i, s)
            vcopies.append(send(
                visual.at[:, pl.ds(pl.multiple_of(t * per, per), per)], vis.at[y, z],
                vsend.at[n], vrecv.at[n], "blk", t))
        vis[y, z] = visual[:, pl.ds(pl.multiple_of(b * per, per), per)]

    stores = []

    def attention(j):
        block = kv[j].reshape(nb * ROWS, 2 * D)
        k, v = block[:, :D], block[:, D:]
        k_t, v_t = k.T, v.T
        dk = dv = None
        for p in range(GROUP // 2):
            cols = [slice(j * SPAN + (2 * p + i) * D, j * SPAN + (2 * p + i + 1) * D) for i in (0, 1)]
            q = jnp.concatenate([q_ref[:, c] for c in cols], axis=0)
            g = jnp.concatenate([g_ref[:, c] for c in cols], axis=0)
            g_t = g.T
            s = dot(k, q, ((1,), (1,))) + bias[...]
            peak = jnp.max(s, axis=0, keepdims=True)
            e = jnp.exp2((s - peak) * EXP2_SCALE)
            probs = e * (1.0 / jnp.sum(e, axis=0, keepdims=True))
            w = probs.astype(BF16)
            o_t = dot(v_t, w, ((1,), (0,))).astype(BF16).astype(F32)
            delta = jnp.sum(g_t.astype(F32) * o_t, axis=0, keepdims=True)
            dp = dot(v, g_t, ((1,), (0,)))
            ds = (probs * ((dp - delta) * SCALE)).astype(BF16)
            dq_t = dot(k_t, ds, ((1,), (0,)))
            o = o_t.T.astype(BF16)
            dq = dq_t.T.astype(BF16)
            for i in (0, 1):
                o_ref[:, cols[i]] = o[i * D:(i + 1) * D]
                dq_ref[:, cols[i]] = dq[i * D:(i + 1) * D]
            dv_p = dot(w, g, ((1,), (0,)))
            dk_p = dot(ds, q, ((1,), (0,)))
            dv = dv_p if dv is None else dv + dv_p
            dk = dk_p if dk is None else dk + dk_p
        part[j, :, :, :, :D] = dk.astype(BF16).reshape(2, nz, ROWS, D)
        part[j, :, :, :, D:] = dv.astype(BF16).reshape(2, nz, ROWS, D)
        cols = pl.ds(j * SPAN, SPAN)
        for i, (src, dst) in enumerate(((o_ref, o_hbm), (dq_ref, dq_hbm))):
            c = pltpu.make_async_copy(src.at[:, cols], dst.at[:, cols], store.at[i, j])
            c.start()
            stores.append(c)

    ycopies, hcopies, kcopies, wcopies = {}, {}, {}, {}

    def swap(j):
        ycopies[j] = send(part.at[j, 1 - y], yin.at[j], ysend.at[j], yrecv.at[j], "blk", partner)

    def scatter(j):
        ycopies[j].wait_recv()
        half[j] = (part[j, y].astype(F32) + yin[j].astype(F32)).astype(BF16)
        for i in near_first(nz):
            hcopies[j, i] = send(half.at[j, zmod(i)], zin.at[j, i - 1],
                                 hsend.at[j, i - 1], hrecv.at[j, i - 1], "blk", zpeer(i))

    def collect(j):
        total = half[j, z].astype(F32)
        for i in near_first(nz):
            hcopies[j, i].wait_recv()
            total += zin[j, i - 1].astype(F32)
        kg[j, y, z] = total[:, :D].astype(BF16)
        ref = kg.at[j, y, z]
        for n, (i, s) in enumerate(peers):
            kcopies[j, n] = send(ref, ref, ksend.at[j, n], krecv.at[j, n], "blk", at(i, s))
        dv_out[:, j * D:(j + 1) * D] = total[:, D:].astype(BF16)

    def weight_term(j, vis_t):
        for n in range(len(peers)):
            kcopies[j, n].wait_recv()
        term = dot(vis_t, kg[j].reshape(nb * ROWS, D), ((1,), (0,)))
        wpart[j] = term.astype(BF16).reshape(nd, per // nd, D)
        for i in range(1, nd):
            t = lax.rem(d + i, nd)
            wcopies[j, i] = send(wpart.at[j, t], landed.at[j, i - 1],
                                 wsend.at[j, i - 1], wrecv.at[j, i - 1], "dp", t)

    def weight_sum(j):
        total = wpart[j, d].astype(F32)
        for i in range(1, nd):
            wcopies[j, i].wait_recv()
            total += landed[j, i - 1].astype(F32)
        dw_out[:, j * D:(j + 1) * D] = total

    loads[0].wait()
    loads[1].wait()
    project(0)
    pl.semaphore_wait(barrier, len(peers) + nd - 1)
    gather(0)
    for j in range(1, HEADS):
        project(j)
        gather(j)
    forward(0)
    forward(1)
    loads[2].wait()
    loads[3].wait()
    arrive(0)
    attention(0)
    swap(0)
    forward(2)
    forward(3)
    exchange()
    arrive(1)
    attention(1)
    swap(1)
    scatter(0)
    arrive(2)
    attention(2)
    swap(2)
    scatter(1)
    collect(0)
    arrive(3)
    attention(3)
    swap(3)
    scatter(2)
    collect(1)
    for c in vcopies:
        c.wait_recv()
    vis_t = vis[...].reshape(nb * ROWS, per).T
    weight_term(0, vis_t)
    scatter(3)
    collect(2)
    weight_term(1, vis_t)
    collect(3)
    weight_term(2, vis_t)
    weight_sum(0)
    weight_sum(1)
    weight_term(3, vis_t)
    weight_sum(2)
    weight_sum(3)
    for c in sent:
        c.wait_send()
    for c in stores:
        c.wait()


def local(visual_rows, value_matrix, key_weight, queries, output_gradient, visual_len, frame_end):
    nb, nd = lax.axis_size("blk"), lax.axis_size("dp")
    nz = nb // 2
    width = HEADS * D
    features = visual_rows.shape[2]
    per = features // nb
    text = queries.shape[1]
    columns = queries.shape[2]
    dma = pltpu.SemaphoreType.DMA
    smem = pl.BlockSpec(memory_space=pltpu.SMEM)
    vmem = pl.BlockSpec(memory_space=pltpu.VMEM)
    hbm = pl.BlockSpec(memory_space=pl.ANY)

    def pair(*shape):
        return [dma(shape), dma(shape)]

    attn_out, query_grad, value_grad, weight_grad = pl.pallas_call(
        kernel,
        out_shape=(
            jax.ShapeDtypeStruct((text, columns), BF16),
            jax.ShapeDtypeStruct((text, columns), BF16),
            jax.ShapeDtypeStruct((ROWS, width), BF16),
            jax.ShapeDtypeStruct((per // nd, width), F32),
        ),
        in_specs=[smem] * 2 + [hbm] * 5,
        out_specs=(hbm, hbm, vmem, vmem),
        scratch_shapes=[
            pltpu.VMEM((ROWS, features), BF16),
            pltpu.VMEM((ROWS, width), BF16),
            pltpu.VMEM((features, width), BF16),
            pltpu.VMEM((text, columns), BF16),
            pltpu.VMEM((text, columns), BF16),
            pltpu.VMEM((text, columns), BF16),
            pltpu.VMEM((text, columns), BF16),
            pltpu.VMEM((nb * ROWS, 2 * D), F32),
            pltpu.VMEM((HEADS, 2, nz, ROWS, 2 * D), BF16),
            pltpu.VMEM((HEADS, 2, nz, ROWS, 2 * D), BF16),
            pltpu.VMEM((HEADS, nz, ROWS, 2 * D), BF16),
            pltpu.VMEM((HEADS, nz, ROWS, 2 * D), BF16),
            pltpu.VMEM((HEADS, nz - 1, ROWS, 2 * D), BF16),
            pltpu.VMEM((HEADS, 2, nz, ROWS, D), BF16),
            pltpu.VMEM((2, nz, ROWS, per), BF16),
            pltpu.VMEM((HEADS, nd, per // nd, D), BF16),
            pltpu.VMEM((HEADS, nd - 1, per // nd, D), BF16),
            dma((4,)), dma((HEADS,)), dma((2, HEADS)),
            *pair(HEADS, nz - 1), *pair(HEADS, nz), *pair(nb - 1),
            *pair(HEADS), *pair(HEADS, nz - 1), *pair(HEADS, nb - 1), *pair(HEADS, nd - 1),
        ],
        compiler_params=pltpu.CompilerParams(
            collective_id=0, has_side_effects=True, vmem_limit_bytes=56 << 20),
        name="cross_attention",
    )(visual_len, frame_end, visual_rows[0], value_matrix[0], key_weight, queries[0], output_gradient[0])
    return attn_out[None], query_grad[None], value_grad[None], weight_grad


def solution(mesh):
    return jax.shard_map(
        local,
        mesh=mesh,
        in_specs=(
            P("dp", "blk", None),
            P("dp", "blk", None),
            P(),
            P("dp", "blk", None),
            P("dp", "blk", None),
            P("dp"),
            P("dp", None),
        ),
        out_specs=(
            P("dp", "blk", None),
            P("dp", "blk", None),
            P("dp", "blk", None),
            P(("blk", "dp"), None),
        ),
        check_vma=False,
    )
```

time: 1640 us -> 82.7 us (0.05)
  waiting for transfers between devices: 1560 us -> 0 us
  Pallas kernels: 0 us -> 75.4 us
  matrix products: 31.2 us -> 0 us
  local copies, waits for them, and re-layouts: 23.5 us -> 5.82 us
    unnamed x4 -> x0, waiting for transfers between devices: 1280 us -> none
    reduce_scatter x1 -> x0, waiting for transfers between devices: 200 us -> none  [local(): lax.psum_scatter(row_sums.astype(jnp.bfloat16), 'blk', scatter_dimension=...]
    pallas_call x0 -> x1, Pallas kernels: none -> 75.4 us  [local(): pl.pallas_call(kernel, out_shape=(jax.ShapeDtypeStruct((text, columns), B...]
    all_gather x1 -> x0, waiting for transfers between devices: 73 us -> none  [local(): gathered = lax.all_gather(key_values, 'blk', axis=0, tiled=True)]
    dot_general x7 -> x0, matrix products: 23.3 us -> none  [the longest x1 5.71 us: local(): jnp.einsum('tkgd,rkd->kgrt', gradient_rows, value_portion, preferred_elem...]
  transfers between devices with their start and end apart: 3 -> 0, of which waited for: 3 -> 0; matrix products, arithmetic and copies ran while one was open for 1% -> 0% of each run, Pallas kernels for 0% -> 0%
where the time goes in v2:
time: 82.7 us; the launch traced here: 82.5 us
  Pallas kernels  75.4 us (91%)
  local copies, waits for them, and re-layouts  5.82 us (7%)
  between operations  1.31 us (2%)
    pallas_call x1, Pallas kernels, local(): pl.pallas_call(kernel, out_shape=(jax.ShapeDtypeStruct((text, columns), B...  75.4 us
    unnamed x8, local copies, waits for them, and re-layouts  5.82 us

profile of v2, /device:TPU:1, one launch (start us, length us, event | category | flops | bytes accessed | tf_op | source)
XLA Modules:
  0.0 82.5 jit_solution(4907480719812253209)
XLA Ops:
  1.3 75.4 %cross_attention.1 = (bf16[128,4096]{1,0:T(8,128)(2,1)}, bf16[128,4096]{1,0:T(8,128)(2,1)}, bf16[32,512]{1,0:T(8,128)(2,1)}, f32[16,512]{1,0:T(8,128)}) custom-call(s32[1]{0:T(128)S(6)} %copy.15.length, s32[1,16]{1,0:T(1,128)} %frames.1, bf16[32,4096]{1,0:T(8,128)(2,1)} %bitcast.11, bf16[32,512]{1,0:T(8,128)(2,1)} %bitcast.12, bf16[4096,512]{1,0:T(8,128)(2,1)} %weight_hbm.1, ...), custom_call_target="tpu_custom_call" | custom-call | tf_op jit(solution)/shard_map/cross_attention/pallas_call | solution.py:276
  76.7 0.0 copy-start.1
  76.7 0.0 copy-start
  76.7 2.3 %copy.16 = bf16[1,128,4096]{2,1,0:T(8,128)(2,1)} copy(bf16[1,128,4096]{2,1,0:T(8,128)(2,1)} %bitcast.8) | data formatting | bytes 2097152
  79.0 2.3 %copy.17 = bf16[1,128,4096]{2,1,0:T(8,128)(2,1)} copy(bf16[1,128,4096]{2,1,0:T(8,128)(2,1)} %bitcast.7) | data formatting | bytes 2097152
  81.3 0.0 copy-done.1
  81.3 0.6 copy.18
  81.9 0.0 copy-done
  81.9 0.6 copy.19
Async XLA Ops:
  76.7 4.6 %copy-start.1 = (bf16[32,512]{1,0:T(8,128)(2,1)S(1)}, bf16[32,512]{1,0:T(8,128)(2,1)}, u32[]{:S(2)}) copy-start(bf16[32,512]{1,0:T(8,128)(2,1)} %get-tuple-element.10) | copy-start | bytes 98308
  76.7 5.2 %copy-start = (f32[16,512]{1,0:T(8,128)S(1)}, f32[16,512]{1,0:T(8,128)}, u32[]{:S(2)}) copy-start(f32[16,512]{1,0:T(8,128)} %get-tuple-element.19) | copy-start | bytes 98308

commit v3 on v2

v3 whole, which is shorter than its diff:
```python
import math

import jax
import jax.numpy as jnp
from jax import lax
from jax.experimental import pallas as pl
from jax.experimental.pallas import tpu as pltpu
from jax.sharding import PartitionSpec as P

HEADS = 4
GROUP = 8
D = 128
SPAN = GROUP * D
TILE = 128
ROWS = 32
SCALE = D ** (-0.5)
EXP2_SCALE = SCALE * math.log2(math.e)
FILLER = -1e30
MESH = pl.DeviceIdType.MESH
F32 = jnp.float32
BF16 = jnp.bfloat16


def dot(a, b, dims):
    return lax.dot_general(a, b, (dims, ((), ())), preferred_element_type=F32)


def near_first(n):
    return sorted(range(1, n), key=lambda i: min(i, n - i))


def kernel(length, frames, visual_hbm, values_hbm, weight_hbm, queries_hbm, grads_hbm,
           o_ref, dq_ref, dv_out, dw_out,
           visual, values, weight, q_ref, g_ref, bias,
           kv, w_all, ds_all, o_all, part, yin, half, zin, direct, vpart, vyin, vhalf, vzin,
           kg, vis, wpart, landed,
           load, weight_load, out_sem, zrecv, frecv, vrecv,
           yrecv, hrecv, drecv, vyrecv, vhrecv, krecv, wrecv):
    b = lax.axis_index("blk")
    d = lax.axis_index("dp")
    nb, nd = lax.axis_size("blk"), lax.axis_size("dp")
    nz = nb // 2
    z, y = b // 2, b % 2
    per = visual.shape[1] // nb

    def zmod(i):
        return lax.rem(z + i, nz)

    def zpeer(i):
        return zmod(i) * 2 + y

    partner = b + 1 - 2 * y
    peers = [(i, s) for i in [0] + near_first(nz) for s in (0, 1) if i or s]
    sent = []

    def send(src, dst, rsem, axis, index):
        c = pltpu.make_async_remote_copy(
            src_ref=src, dst_ref=dst, send_sem=out_sem, recv_sem=rsem,
            device_id={axis: index}, device_id_type=MESH)
        c.start()
        sent.append(math.prod(src.shape))
        return c

    def wait_for(sem, elements):
        width = weight.shape[1] if elements % (16 * weight.shape[1]) == 0 else D
        ref = weight.at[pl.ds(0, elements // width), pl.ds(0, width)]
        pltpu.make_async_copy(ref, ref, sem).wait()

    def side(s):
        return y if s == 0 else 1 - y

    def at(i, s):
        return zmod(i) * 2 + side(s)

    loads = []
    for i, (src, dst) in enumerate(((visual_hbm, visual), (values_hbm, values))):
        loads.append(pltpu.make_async_copy(src, dst, load.at[i]))
        loads[-1].start()
    wloads = []
    for j in range(HEADS):
        cols = pl.ds(j * D, D)
        wloads.append(pltpu.make_async_copy(weight_hbm.at[:, cols], weight.at[:, cols], weight_load.at[j]))
        wloads[-1].start()
    for i, (src, dst) in enumerate(((queries_hbm, q_ref), (grads_hbm, g_ref))):
        loads.append(pltpu.make_async_copy(src, dst, load.at[2 + i]))
        loads[-1].start()

    barrier = pltpu.get_barrier_semaphore()
    line = [zpeer(i) for i in range(1, nz)] + [partner]
    for t in line:
        pl.semaphore_signal(barrier, inc=1, device_id={"blk": t}, device_id_type=MESH)
    for i in range(1, nd):
        pl.semaphore_signal(barrier, inc=1, device_id={"dp": lax.rem(d + i, nd)}, device_id_type=MESH)

    limit = jnp.minimum(length[0], TILE * frames[0, b])
    r = lax.broadcasted_iota(jnp.int32, bias.shape, 0)
    row = ((r & (nz * ROWS - 1)) // ROWS) * (2 * ROWS) + (r // (nz * ROWS)) * ROWS + (r & (ROWS - 1))
    bias[...] = jnp.where(row < limit, 0.0, FILLER)

    zcopies, fcopies = {}, {}

    def project(j):
        wloads[j].wait()
        cols = slice(j * D, (j + 1) * D)
        key = jnp.dot(visual[...], weight[:, cols], preferred_element_type=F32)
        kv[j, y, z, :, :D] = key.astype(BF16)
        kv[j, y, z, :, D:] = values[:, cols]

    def gather(j):
        ref = kv.at[j, y, z]
        fcopies[j, 0] = send(ref, ref, frecv.at[j], "blk", partner)
        for i in near_first(nz):
            zcopies[j, i] = send(ref, ref, zrecv.at[j, i - 1], "blk", zpeer(i))

    def forward(j):
        for i in near_first(nz):
            zcopies[j, i].wait_recv()
            ref = kv.at[j, y, zmod(nz - i)]
            fcopies[j, i] = send(ref, ref, frecv.at[j], "blk", partner)

    def arrive(j):
        wait_for(frecv.at[j], nz * ROWS * 2 * D)

    def exchange():
        for i, s in peers:
            t = at(i, s)
            send(visual.at[:, pl.ds(pl.multiple_of(t * per, per), per)], vis.at[y, z], vrecv, "blk", t)
        vis[y, z] = visual[:, pl.ds(pl.multiple_of(b * per, per), per)]

    def stack(ref, j, first, count):
        at0 = j * SPAN + first * D
        return jnp.concatenate([ref[:, at0 + i * D:at0 + (i + 1) * D] for i in range(count)], axis=0)

    def rows_of(j):
        block = kv[j].reshape(nb * ROWS, 2 * D)
        return block[:, :D], block[:, D:]

    def attention(j):
        k, v = rows_of(j)
        v_t = v.T
        for p in range(GROUP // 2):
            cols = slice(2 * p * D, (2 * p + 2) * D)
            q = stack(q_ref, j, 2 * p, 2)
            g_t = stack(g_ref, j, 2 * p, 2).T
            s = dot(k, q, ((1,), (1,))) + bias[...]
            peak = jnp.max(s, axis=0, keepdims=True)
            e = jnp.exp2((s - peak) * EXP2_SCALE)
            probs = e * (1.0 / jnp.sum(e, axis=0, keepdims=True))
            w = probs.astype(BF16)
            w_all[j, :, cols] = w
            o_t = dot(v_t, w, ((1,), (0,))).astype(BF16)
            o_all[j, :, cols] = o_t
            delta = jnp.sum(g_t.astype(F32) * o_t.astype(F32), axis=0, keepdims=True)
            dp = dot(v, g_t, ((1,), (0,)))
            ds_all[j, :, cols] = (probs * ((dp - delta) * SCALE)).astype(BF16)
        dk = dot(ds_all[j], stack(q_ref, j, 0, GROUP), ((1,), (0,)))
        part[j] = dk.astype(BF16).reshape(2, nz, ROWS, D)

    def finish(j):
        k, _ = rows_of(j)
        dv = dot(w_all[j], stack(g_ref, j, 0, GROUP), ((1,), (0,)))
        vpart[j // 2, :, :, :, (j % 2) * D:(j % 2 + 1) * D] = dv.astype(BF16).reshape(2, nz, ROWS, D)
        dq_t = dot(k.T, ds_all[j], ((1,), (0,)))
        for i in range(GROUP):
            cols = slice(j * SPAN + i * D, j * SPAN + (i + 1) * D)
            o_ref[:, cols] = o_all[j, :, i * D:(i + 1) * D].T
            dq_ref[:, cols] = dq_t[:, i * D:(i + 1) * D].T.astype(BF16)

    def swap(j):
        send(part.at[j, 1 - y], yin.at[j], yrecv.at[j], "blk", partner)

    def scatter(j):
        wait_for(yrecv.at[j], nz * ROWS * D)
        half[j] = (part[j, y].astype(F32) + yin[j].astype(F32)).astype(BF16)
        for i in near_first(nz):
            send(half.at[j, zmod(i)], zin.at[j, i - 1], hrecv.at[j], "blk", zpeer(i))

    def publish(j, total):
        kg[j, y, z] = total.astype(BF16)
        ref = kg.at[j, y, z]
        for i, s in peers:
            send(ref, ref, krecv.at[j], "blk", at(i, s))

    def collect(j):
        wait_for(hrecv.at[j], (nz - 1) * ROWS * D)
        total = half[j, z].astype(F32)
        for i in range(1, nz):
            total += zin[j, i - 1].astype(F32)
        publish(j, total)

    def spread(j):
        for n, (i, s) in enumerate(peers):
            send(part.at[j, side(s), zmod(i)], direct.at[n], drecv, "blk", at(i, s))

    def collect_direct(j):
        wait_for(drecv, len(peers) * ROWS * D)
        total = part[j, y, z].astype(F32)
        for n in range(len(peers)):
            total += direct[n].astype(F32)
        publish(j, total)

    def vswap(h):
        send(vpart.at[h, 1 - y], vyin.at[h], vyrecv.at[h], "blk", partner)

    def vscatter(h):
        wait_for(vyrecv.at[h], nz * ROWS * 2 * D)
        vhalf[h] = (vpart[h, y].astype(F32) + vyin[h].astype(F32)).astype(BF16)
        for i in near_first(nz):
            send(vhalf.at[h, zmod(i)], vzin.at[h, i - 1], vhrecv.at[h], "blk", zpeer(i))

    def vcollect(h):
        wait_for(vhrecv.at[h], (nz - 1) * ROWS * 2 * D)
        total = vhalf[h, z].astype(F32)
        for i in range(1, nz):
            total += vzin[h, i - 1].astype(F32)
        dv_out[:, h * 2 * D:(h + 1) * 2 * D] = total.astype(BF16)

    def weight_term(j, vis_t):
        wait_for(krecv.at[j], len(peers) * ROWS * D)
        term = dot(vis_t, kg[j].reshape(nb * ROWS, D), ((1,), (0,)))
        wpart[j] = term.astype(BF16).reshape(nd, per // nd, D)
        for i in range(1, nd):
            t = lax.rem(d + i, nd)
            send(wpart.at[j, t], landed.at[j, i - 1], wrecv.at[j], "dp", t)

    def weight_sum(j):
        wait_for(wrecv.at[j], (nd - 1) * wpart.shape[2] * D)
        total = wpart[j, d].astype(F32)
        for i in range(1, nd):
            total += landed[j, i - 1].astype(F32)
        dw_out[:, j * D:(j + 1) * D] = total

    loads[0].wait()
    loads[1].wait()
    project(0)
    pl.semaphore_wait(barrier, len(line) + nd - 1)
    gather(0)
    for j in range(1, HEADS):
        project(j)
        gather(j)
    forward(0)
    forward(1)
    loads[2].wait()
    loads[3].wait()
    arrive(0)
    attention(0)
    swap(0)
    forward(2)
    forward(3)
    arrive(1)
    exchange()
    attention(1)
    swap(1)
    scatter(0)
    arrive(2)
    attention(2)
    swap(2)
    scatter(1)
    arrive(3)
    attention(3)
    spread(3)
    collect(0)
    scatter(2)
    finish(0)
    finish(1)
    vswap(0)
    collect(1)
    finish(2)
    finish(3)
    vswap(1)
    collect(2)
    wait_for(vrecv, len(peers) * ROWS * per)
    vis_t = vis[...].reshape(nb * ROWS, per).T
    collect_direct(3)
    vscatter(0)
    weight_term(0, vis_t)
    weight_term(1, vis_t)
    vscatter(1)
    weight_term(2, vis_t)
    weight_term(3, vis_t)
    vcollect(0)
    vcollect(1)
    weight_sum(0)
    weight_sum(1)
    weight_sum(2)
    weight_sum(3)
    wait_for(out_sem, sum(sent))


def local(visual_rows, value_matrix, key_weight, queries, output_gradient, visual_len, frame_end):
    nb, nd = lax.axis_size("blk"), lax.axis_size("dp")
    nz = nb // 2
    width = HEADS * D
    features = visual_rows.shape[2]
    per = features // nb
    text = queries.shape[1]
    columns = queries.shape[2]
    dma = pltpu.SemaphoreType.DMA
    smem = pl.BlockSpec(memory_space=pltpu.SMEM)
    vmem = pl.BlockSpec(memory_space=pltpu.VMEM)
    hbm = pl.BlockSpec(memory_space=pltpu.HBM)

    attn_out, query_grad, value_grad, weight_grad = pl.pallas_call(
        kernel,
        out_shape=(
            pltpu.VMEM((text, columns), BF16),
            pltpu.VMEM((text, columns), BF16),
            pltpu.VMEM((ROWS, width), BF16),
            pltpu.VMEM((per // nd, width), F32),
        ),
        in_specs=[smem] * 2 + [hbm] * 5,
        out_specs=(vmem,) * 4,
        scratch_shapes=[
            pltpu.VMEM((ROWS, features), BF16),
            pltpu.VMEM((ROWS, width), BF16),
            pltpu.VMEM((features, width), BF16),
            pltpu.VMEM((text, columns), BF16),
            pltpu.VMEM((text, columns), BF16),
            pltpu.VMEM((nb * ROWS, 2 * D), F32),
            pltpu.VMEM((HEADS, 2, nz, ROWS, 2 * D), BF16),
            pltpu.VMEM((HEADS, nb * ROWS, SPAN), BF16),
            pltpu.VMEM((HEADS, nb * ROWS, SPAN), BF16),
            pltpu.VMEM((HEADS, D, SPAN), BF16),
            pltpu.VMEM((HEADS, 2, nz, ROWS, D), BF16),
            pltpu.VMEM((HEADS, nz, ROWS, D), BF16),
            pltpu.VMEM((HEADS, nz, ROWS, D), BF16),
            pltpu.VMEM((HEADS, nz - 1, ROWS, D), BF16),
            pltpu.VMEM((nb - 1, ROWS, D), BF16),
            pltpu.VMEM((2, 2, nz, ROWS, 2 * D), BF16),
            pltpu.VMEM((2, nz, ROWS, 2 * D), BF16),
            pltpu.VMEM((2, nz, ROWS, 2 * D), BF16),
            pltpu.VMEM((2, nz - 1, ROWS, 2 * D), BF16),
            pltpu.VMEM((HEADS, 2, nz, ROWS, D), BF16),
            pltpu.VMEM((2, nz, ROWS, per), BF16),
            pltpu.VMEM((HEADS, nd, per // nd, D), BF16),
            pltpu.VMEM((HEADS, nd - 1, per // nd, D), BF16),
            dma((4,)), dma((HEADS,)), dma, dma((HEADS, nz - 1)), dma((HEADS,)), dma,
            dma((HEADS,)), dma((HEADS,)), dma, dma((2,)), dma((2,)), dma((HEADS,)), dma((HEADS,)),
        ],
        compiler_params=pltpu.CompilerParams(
            collective_id=0, has_side_effects=True, vmem_limit_bytes=63000 << 10),
        name="cross_attention",
    )(visual_len, frame_end, visual_rows[0], value_matrix[0], key_weight, queries[0], output_gradient[0])
    return attn_out[None], query_grad[None], value_grad[None], weight_grad


def solution(mesh):
    return jax.shard_map(
        local,
        mesh=mesh,
        in_specs=(
            P("dp", "blk", None),
            P("dp", "blk", None),
            P(),
            P("dp", "blk", None),
            P("dp", "blk", None),
            P("dp"),
            P("dp", None),
        ),
        out_specs=(
            P("dp", "blk", None),
            P("dp", "blk", None),
            P("dp", "blk", None),
            P(("blk", "dp"), None),
        ),
        check_vma=False,
    )
```

time: 82.7 us -> 66.9 us (0.81)
  Pallas kernels: 75.4 us -> 62.3 us
  local copies, waits for them, and re-layouts: 5.82 us -> 3.17 us
    pallas_call x1, Pallas kernels: 75.4 us -> 62.3 us  [local(): pl.pallas_call(kernel, out_shape=(pltpu.VMEM((text, columns), BF16), pltp...]
    unnamed x8 -> x4, local copies, waits for them, and re-layouts: 5.82 us -> 3.17 us
where the time goes in v3:
time: 66.9 us; the launch traced here: 66.8 us
  Pallas kernels  62.3 us (93%)
  local copies, waits for them, and re-layouts  3.17 us (5%)
  between operations  1.29 us (2%)
    pallas_call x1, Pallas kernels, local(): pl.pallas_call(kernel, out_shape=(pltpu.VMEM((text, columns), BF16), pltp...  62.3 us
    unnamed x4, local copies, waits for them, and re-layouts  3.17 us

profile of v3, /device:TPU:1, one launch (start us, length us, event | category | flops | bytes accessed | tf_op | source)
XLA Modules:
  0.0 66.8 jit_solution(4373648960767278522)
XLA Ops:
  1.3 62.3 %cross_attention.1 = (bf16[128,4096]{1,0:T(8,128)(2,1)S(1)}, bf16[128,4096]{1,0:T(8,128)(2,1)S(1)}, bf16[32,512]{1,0:T(8,128)(2,1)S(1)}, f32[16,512]{1,0:T(8,128)S(1)}) custom-call(s32[1]{0:T(128)S(6)} %copy.19.length, s32[1,16]{1,0:T(1,128)} %frames.1, bf16[32,4096]{1,0:T(8,128)(2,1)} %bitcast.12, bf16[32,512]{1,0:T(8,128)(2,1)} %bitcast.13, ...), custom_call_target="tpu_custom_call" | custom-call | tf_op jit(solution)/shard_map/cross_attention/pallas_call | solution.py:303
  63.6 1.0 %copy.15 = bf16[1,128,4096]{2,1,0:T(8,128)(2,1)} copy(bf16[1,128,4096]{2,1,0:T(8,128)(2,1)S(1)} %bitcast.8) | data formatting | bytes 2097152
  64.6 1.0 %copy.16 = bf16[1,128,4096]{2,1,0:T(8,128)(2,1)} copy(bf16[1,128,4096]{2,1,0:T(8,128)(2,1)S(1)} %bitcast.7) | data formatting | bytes 2097152
  65.5 0.6 copy.17
  66.2 0.6 copy.18

commit v4 on v3

--- a/solution.py
+++ b/solution.py
@@ -29,13 +29,17 @@
     return sorted(range(1, n), key=lambda i: min(i, n - i))
 
 
+def far_first(n):
+    return near_first(n)[::-1]
+
+
 def kernel(length, frames, visual_hbm, values_hbm, weight_hbm, queries_hbm, grads_hbm,
            o_ref, dq_ref, dv_out, dw_out,
            visual, values, weight, q_ref, g_ref, bias,
            kv, w_all, ds_all, o_all, part, yin, half, zin, direct, vpart, vyin, vhalf, vzin,
            kg, vis, wpart, landed,
            load, weight_load, out_sem, zrecv, frecv, vrecv,
-           yrecv, hrecv, drecv, vyrecv, vhrecv, krecv, wrecv):
+           yrecv, hrecv, drecv, vyrecv, vhrecv, kzrecv, krecv, wrecv):
     b = lax.axis_index("blk")
     d = lax.axis_index("dp")
     nb, nd = lax.axis_size("blk"), lax.axis_size("dp")
@@ -50,7 +54,7 @@
         return zmod(i) * 2 + y
 
     partner = b + 1 - 2 * y
-    peers = [(i, s) for i in [0] + near_first(nz) for s in (0, 1) if i or s]
+    peers = [(i, s) for i in far_first(nz) + [0] for s in (1, 0) if i or s]
     sent = []
 
     def send(src, dst, rsem, axis, index):
@@ -109,7 +113,7 @@
     def gather(j):
         ref = kv.at[j, y, z]
         fcopies[j, 0] = send(ref, ref, frecv.at[j], "blk", partner)
-        for i in near_first(nz):
+        for i in far_first(nz):
             zcopies[j, i] = send(ref, ref, zrecv.at[j, i - 1], "blk", zpeer(i))
 
     def forward(j):
@@ -172,14 +176,23 @@
     def scatter(j):
         wait_for(yrecv.at[j], nz * ROWS * D)
         half[j] = (part[j, y].astype(F32) + yin[j].astype(F32)).astype(BF16)
-        for i in near_first(nz):
+        for i in far_first(nz):
             send(half.at[j, zmod(i)], zin.at[j, i - 1], hrecv.at[j], "blk", zpeer(i))
 
     def publish(j, total):
         kg[j, y, z] = total.astype(BF16)
         ref = kg.at[j, y, z]
-        for i, s in peers:
-            send(ref, ref, krecv.at[j], "blk", at(i, s))
+        if j == HEADS - 1:
+            for i, s in peers:
+                send(ref, ref, krecv.at[j], "blk", at(i, s))
+        else:
+            for i in far_first(nz):
+                send(ref, ref, kzrecv.at[j], "blk", zpeer(i))
+
+    def across(j):
+        wait_for(kzrecv.at[j], (nz - 1) * ROWS * D)
+        ref = kg.at[j, y]
+        send(ref, ref, krecv.at[j], "blk", partner)
 
     def collect(j):
         wait_for(hrecv.at[j], (nz - 1) * ROWS * D)
@@ -205,7 +218,7 @@
     def vscatter(h):
         wait_for(vyrecv.at[h], nz * ROWS * 2 * D)
         vhalf[h] = (vpart[h, y].astype(F32) + vyin[h].astype(F32)).astype(BF16)
-        for i in near_first(nz):
+        for i in far_first(nz):
             send(vhalf.at[h, zmod(i)], vzin.at[h, i - 1], vhrecv.at[h], "blk", zpeer(i))
 
     def vcollect(h):
@@ -216,7 +229,7 @@
         dv_out[:, h * 2 * D:(h + 1) * 2 * D] = total.astype(BF16)
 
     def weight_term(j, vis_t):
-        wait_for(krecv.at[j], len(peers) * ROWS * D)
+        wait_for(krecv.at[j], (len(peers) if j == HEADS - 1 else nz) * ROWS * D)
         term = dot(vis_t, kg[j].reshape(nb * ROWS, D), ((1,), (0,)))
         wpart[j] = term.astype(BF16).reshape(nd, per // nd, D)
         for i in range(1, nd):
@@ -243,12 +256,12 @@
     loads[2].wait()
     loads[3].wait()
     arrive(0)
+    exchange()
     attention(0)
     swap(0)
     forward(2)
     forward(3)
     arrive(1)
-    exchange()
     attention(1)
     swap(1)
     scatter(0)
@@ -256,26 +269,29 @@
     attention(2)
     swap(2)
     scatter(1)
+    collect(0)
     arrive(3)
     attention(3)
     spread(3)
-    collect(0)
     scatter(2)
     finish(0)
     finish(1)
     vswap(0)
     collect(1)
+    across(0)
     finish(2)
     finish(3)
     vswap(1)
     collect(2)
+    across(1)
+    collect_direct(3)
+    across(2)
+    vscatter(0)
     wait_for(vrecv, len(peers) * ROWS * per)
     vis_t = vis[...].reshape(nb * ROWS, per).T
-    collect_direct(3)
-    vscatter(0)
     weight_term(0, vis_t)
+    vscatter(1)
     weight_term(1, vis_t)
-    vscatter(1)
     weight_term(2, vis_t)
     weight_term(3, vis_t)
     vcollect(0)
@@ -335,7 +351,7 @@
             pltpu.VMEM((HEADS, nd, per // nd, D), BF16),
             pltpu.VMEM((HEADS, nd - 1, per // nd, D), BF16),
             dma((4,)), dma((HEADS,)), dma, dma((HEADS, nz - 1)), dma((HEADS,)), dma,
-            dma((HEADS,)), dma((HEADS,)), dma, dma((2,)), dma((2,)), dma((HEADS,)), dma((HEADS,)),
+            dma((HEADS,)), dma((HEADS,)), dma, dma((2,)), dma((2,)), dma((HEADS,)), dma((HEADS,)), dma((HEADS,)),
         ],
         compiler_params=pltpu.CompilerParams(
             collective_id=0, has_side_effects=True, vmem_limit_bytes=63000 << 10),

time: 66.9 us -> 64.4 us (0.963)
  Pallas kernels: 62.3 us -> 59.8 us
    pallas_call x1, Pallas kernels: 62.3 us -> 59.8 us  [local(): pl.pallas_call(kernel, out_shape=(pltpu.VMEM((text, columns), BF16), pltp...]
where the time goes in v4:
time: 64.4 us; the launch traced here: 64.3 us
  Pallas kernels  59.8 us (93%)
  local copies, waits for them, and re-layouts  3.17 us (5%)
  between operations  1.29 us (2%)
    pallas_call x1, Pallas kernels, local(): pl.pallas_call(kernel, out_shape=(pltpu.VMEM((text, columns), BF16), pltp...  59.8 us
    unnamed x4, local copies, waits for them, and re-layouts  3.17 us

profile of v4, /device:TPU:1, one launch (start us, length us, event | category | flops | bytes accessed | tf_op | source)
XLA Modules:
  0.0 64.3 jit_solution(4646476348854618161)
XLA Ops:
  1.3 59.8 %cross_attention.1 = (bf16[128,4096]{1,0:T(8,128)(2,1)S(1)}, bf16[128,4096]{1,0:T(8,128)(2,1)S(1)}, bf16[32,512]{1,0:T(8,128)(2,1)S(1)}, f32[16,512]{1,0:T(8,128)S(1)}) custom-call(s32[1]{0:T(128)S(6)} %copy.19.length, s32[1,16]{1,0:T(1,128)} %frames.1, bf16[32,4096]{1,0:T(8,128)(2,1)} %bitcast.12, bf16[32,512]{1,0:T(8,128)(2,1)} %bitcast.13, ...), custom_call_target="tpu_custom_call" | custom-call | tf_op jit(solution)/shard_map/cross_attention/pallas_call | solution.py:319
  61.1 1.0 %copy.15 = bf16[1,128,4096]{2,1,0:T(8,128)(2,1)} copy(bf16[1,128,4096]{2,1,0:T(8,128)(2,1)S(1)} %bitcast.8) | data formatting | bytes 2097152
  62.1 1.0 %copy.16 = bf16[1,128,4096]{2,1,0:T(8,128)(2,1)} copy(bf16[1,128,4096]{2,1,0:T(8,128)(2,1)S(1)} %bitcast.7) | data formatting | bytes 2097152
  63.1 0.6 copy.17
  63.7 0.6 copy.18
